TPU v7x, 32 devices: a whole 2x2x4 slice. The times are simulated.
32 devices in a mesh: dp: 8 (over y, x, core), tensor: 4 (over z).
Axes of the slice: x: 2, y: 2, z: 4, core: 2. Of those that a mesh axis runs over, the one named last changes fastest.
Arguments:
- tokens: bfloat16 [8192, 2048], P(('dp', 'tensor')), may hold values from -6 to 6
- seq_start: int32 [8192], P('dp'), may hold values from 0 to 8191, as said below
- proj_weight: bfloat16 [2048, 3, 2048], P('dp', None, 'tensor'), may hold values from -0.125 to 0.125
- proj_bias: bfloat16 [3, 8, 256], P(None, 'tensor', 'dp'), may hold values from -3 to 3
- out_weight: bfloat16 [2048, 2048], P('tensor', 'dp'), may hold values from -1.5 to 1.5
- up_weight: bfloat16 [2048, 8192], P('dp', 'tensor'), may hold values from -0.125 to 0.125
- up_bias: bfloat16 [4, 2048], P('tensor', 'dp'), may hold values from -3 to 3
- down_weight: bfloat16 [8192, 2048], P('tensor', 'dp'), may hold values from -0.0625 to 0.0625
- norm_gains: bfloat16 [2, 2048], P(None, ('dp', 'tensor')), may hold values from 0.099609375 to 1.8984375
- biases: bfloat16 [4, 2048], P(None, ('dp', 'tensor')), may hold values from -3 to 3
- cotangent: bfloat16 [8192, 2048], P(('dp', 'tensor')), may hold values from -6 to 6
Outputs:
- output: bfloat16 [8192, 2048], P(('dp', 'tensor'))
- input_grad: float32 [8192, 2048], P(('dp', 'tensor'))
- proj_grad: float32 [2048, 3, 2048], P('dp', None, 'tensor')
- proj_bias_grad: float32 [3, 8, 256], P(None, 'tensor', 'dp')
- out_grad: float32 [2048, 2048], P('tensor', 'dp')
- up_grad: float32 [2048, 8192], P('dp', 'tensor')
- up_bias_grad: float32 [4, 2048], P('tensor', 'dp')
- down_grad: float32 [8192, 2048], P('tensor', 'dp')
- gains_grad: float32 [2, 2048], P(None, ('dp', 'tensor'))
- biases_grad: float32 [4, 2048], P(None, ('dp', 'tensor'))
Inputs may be any that keep to these rules, and one draw needn't show every extreme that they name: seq_start never falls along the tokens, is at most the token's own index, and every sequence lies inside one aligned block of 1024 tokens (the tokens of one index of dp); some block other than the last holds a single sequence of 1024 tokens, the others hold sequences of uneven lengths, and the last token begins a sequence of its own.
All inputs are finite; a program needn't handle non-finite values.
Results may differ from a plain program's by a relative error of at most 0.012.
Values may be sent and summed in bfloat16 or wider, within the bound.
No kernel may reach another device: no remote copies, remote signals or barrier semaphores. Data moves between devices by JAX's collectives and lax.ppermute only.
A program may use at most 192 MiB of HBM per device.

v0:
```python
import jax
import jax.numpy as jnp
from jax import lax
from jax.sharding import PartitionSpec as P

ROT = 64
EPSILON = 1e-05
ROTARY_BASE = 10000.0


def layer_norm(values, gain_row, shift_row):
    centered = values - jnp.mean(values, axis=-1, keepdims=True)
    spread = jnp.mean(centered * centered, axis=-1, keepdims=True)
    return centered * lax.rsqrt(spread + EPSILON) * gain_row + shift_row


def both_norms(values, gain_rows, shift_rows):
    return (
        layer_norm(values, gain_rows[0], shift_rows[0]),
        layer_norm(values, gain_rows[1], shift_rows[1]),
    )


def gelu_exact(inputs):
    return jax.nn.gelu(inputs, approximate=False)


def rotate(values, positions, turn_sign):
    half_rot = ROT // 2
    frequency = ROTARY_BASE ** (-(jnp.arange(half_rot, dtype=jnp.float32) * 2.0) / ROT)
    angles = positions.astype(jnp.float32)[:, None] * frequency[None, :]
    cosine = jnp.cos(angles)[:, None, :]
    sine_term = turn_sign * jnp.sin(angles)[:, None, :]
    first_half = values[..., :half_rot]
    second_half = values[..., half_rot:ROT]
    return jnp.concatenate(
        [
            first_half * cosine - second_half * sine_term,
            second_half * cosine + first_half * sine_term,
            values[..., ROT:],
        ],
        axis=-1,
    )


def masked_scores(query_block, key_rows, starts, block_start, block_rows):
    row_count = key_rows.shape[0]
    score_scale = key_rows.shape[-1] ** (-0.5)
    key_index = jnp.arange(row_count, dtype=jnp.int32)
    query_begin = lax.dynamic_slice_in_dim(starts, block_start, block_rows, 0)
    query_index = block_start + jnp.arange(block_rows, dtype=jnp.int32)
    scores = (
        jnp.einsum("qhe,khe->hqk", query_block, key_rows, preferred_element_type=jnp.float32)
        * score_scale
    )
    allowed = (query_begin[:, None] == starts[None, :]) & (
        key_index[None, :] <= query_index[:, None]
    )
    return jnp.where(allowed[None], scores, -1e30)


def attention_forward(queries, key_rows, value_rows, starts, block_rows):
    row_count = queries.shape[0]

    def one_block(block_start):
        query_block = lax.dynamic_slice_in_dim(queries, block_start, block_rows, 0)
        scores = masked_scores(query_block, key_rows, starts, block_start, block_rows)
        row_max = jnp.max(scores, axis=-1, keepdims=True)
        powers = jnp.exp(scores - row_max)
        row_total = jnp.sum(powers, axis=-1, keepdims=True)
        weights = (powers / row_total).astype(jnp.bfloat16)
        attended = jnp.einsum(
            "hqk,khe->qhe", weights, value_rows, preferred_element_type=jnp.float32
        )
        return (attended, (row_max + jnp.log(row_total))[..., 0])

    block_starts = jnp.arange(row_count // block_rows, dtype=jnp.int32) * block_rows
    attended, log_total = lax.map(one_block, block_starts)
    return (attended.reshape(queries.shape), log_total)


def attention_backward(queries, key_rows, value_rows, starts, log_total, grad_attended, block_rows):
    row_count = queries.shape[0]
    score_scale = queries.shape[-1] ** (-0.5)

    def one_block(accumulated, pieces):
        block_start, block_total = pieces
        grad_keys, grad_values = accumulated
        query_block = lax.dynamic_slice_in_dim(queries, block_start, block_rows, 0)
        grad_block = lax.dynamic_slice_in_dim(grad_attended, block_start, block_rows, 0)
        scores = masked_scores(query_block, key_rows, starts, block_start, block_rows)
        probs = jnp.exp(scores - block_total[..., None])
        grad_values = grad_values + jnp.einsum(
            "hqk,qhe->khe",
            probs.astype(jnp.bfloat16),
            grad_block,
            preferred_element_type=jnp.float32,
        )
        grad_probs = jnp.einsum(
            "qhe,khe->hqk", grad_block, value_rows, preferred_element_type=jnp.float32
        )
        inner_sum = jnp.sum(probs * grad_probs, axis=-1, keepdims=True)
        grad_scores = (probs * (grad_probs - inner_sum)).astype(jnp.bfloat16)
        grad_query = (
            jnp.einsum("hqk,khe->qhe", grad_scores, key_rows, preferred_element_type=jnp.float32)
            * score_scale
        )
        grad_keys = (
            grad_keys
            + jnp.einsum(
                "hqk,qhe->khe", grad_scores, query_block, preferred_element_type=jnp.float32
            )
            * score_scale
        )
        return ((grad_keys, grad_values), grad_query)

    block_starts = jnp.arange(row_count // block_rows, dtype=jnp.int32) * block_rows
    zeros_like_keys = jnp.zeros(queries.shape, jnp.float32)
    (grad_keys, grad_values), grad_queries = lax.scan(
        one_block, (zeros_like_keys, zeros_like_keys), (block_starts, log_total)
    )
    return (grad_queries.reshape(queries.shape), grad_keys, grad_values)


def shards(
    tokens,
    seq_start,
    proj_weight,
    proj_bias,
    out_weight,
    up_weight,
    up_bias,
    down_weight,
    norm_gains,
    biases,
    cotangent,
):
    local_rows = tokens.shape[0]
    row_count = local_rows * lax.axis_size("tensor")
    block_rows = min(512, row_count)
    dp_index = lax.axis_index("dp")
    gathered = (
        lax.all_gather(proj_weight, "dp", axis=0, tiled=True),
        lax.all_gather(proj_bias, "dp", axis=2, tiled=True),
        lax.all_gather(out_weight, "dp", axis=1, tiled=True),
        lax.all_gather(up_weight, "dp", axis=0, tiled=True),
        lax.all_gather(up_bias, "dp", axis=1, tiled=True),
        lax.all_gather(down_weight, "dp", axis=1, tiled=True),
    )
    joined_weight, joined_bias, mix_weight, hidden_weight, hidden_bias, back_weight = gathered
    gain_rows, shift_rows = (
        lax.all_gather(norm_gains, ("dp", "tensor"), axis=1, tiled=True),
        lax.all_gather(biases, ("dp", "tensor"), axis=1, tiled=True),
    )
    gain_rows = gain_rows.astype(jnp.float32)
    shift_rows = shift_rows.astype(jnp.float32)
    local_f = tokens.astype(jnp.float32)
    first_local, second_local = both_norms(local_f, gain_rows, shift_rows)
    first_rows, second_rows = (
        lax.all_gather(first_local.astype(jnp.bfloat16), "tensor", axis=0, tiled=True),
        lax.all_gather(second_local.astype(jnp.bfloat16), "tensor", axis=0, tiled=True),
    )
    heads_here = joined_bias.shape[1]
    head_size = joined_bias.shape[2]
    local_width = heads_here * head_size
    projected = jnp.einsum(
        "nd,dch->nch", first_rows, joined_weight, preferred_element_type=jnp.float32
    ) + joined_bias.astype(jnp.float32).reshape(3, local_width)
    positions = dp_index * row_count + jnp.arange(row_count, dtype=jnp.int32) - seq_start
    queries = rotate(
        projected[:, 0].reshape(row_count, heads_here, head_size), positions, 1.0
    ).astype(jnp.bfloat16)
    key_rows = rotate(
        projected[:, 1].reshape(row_count, heads_here, head_size), positions, 1.0
    ).astype(jnp.bfloat16)
    value_rows = projected[:, 2].reshape(row_count, heads_here, head_size).astype(jnp.bfloat16)
    attended, log_total = attention_forward(queries, key_rows, value_rows, seq_start, block_rows)
    attended = attended.reshape(row_count, local_width).astype(jnp.bfloat16)
    hidden = jnp.dot(
        second_rows, hidden_weight, preferred_element_type=jnp.float32
    ) + hidden_bias.astype(jnp.float32)
    activated = gelu_exact(hidden).astype(jnp.bfloat16)
    attn_part = jnp.dot(attended, mix_weight, preferred_element_type=jnp.float32)
    branches = lax.psum_scatter(
        attn_part + jnp.dot(activated, back_weight, preferred_element_type=jnp.float32),
        "tensor",
        scatter_dimension=0,
        tiled=True,
    )
    output = (local_f + branches + shift_rows[2] + shift_rows[3]).astype(jnp.bfloat16)
    grad_rows = lax.all_gather(cotangent, "tensor", axis=0, tiled=True)
    regathered = (
        lax.all_gather(proj_weight, "dp", axis=0, tiled=True),
        lax.all_gather(proj_bias, "dp", axis=2, tiled=True),
        lax.all_gather(out_weight, "dp", axis=1, tiled=True),
        lax.all_gather(up_weight, "dp", axis=0, tiled=True),
        lax.all_gather(up_bias, "dp", axis=1, tiled=True),
        lax.all_gather(down_weight, "dp", axis=1, tiled=True),
    )
    joined_again, _, mix_again, hidden_again, _, back_again = regathered
    grad_active = jnp.einsum("nd,fd->nf", grad_rows, back_again, preferred_element_type=jnp.float32)
    down_term = jnp.einsum("nf,nd->fd", activated, grad_rows, preferred_element_type=jnp.float32)
    _, gelu_back = jax.vjp(gelu_exact, hidden)
    grad_hidden = gelu_back(grad_active)[0].astype(jnp.bfloat16)
    up_term = jnp.einsum("nd,nf->df", second_rows, grad_hidden, preferred_element_type=jnp.float32)
    up_bias_term = jnp.sum(grad_hidden, axis=0, keepdims=True, dtype=jnp.float32)
    grad_second = jnp.einsum(
        "nf,df->nd", grad_hidden, hidden_again, preferred_element_type=jnp.float32
    )
    grad_attended = jnp.einsum(
        "nd,ed->ne", grad_rows, mix_again, preferred_element_type=jnp.float32
    ).astype(jnp.bfloat16)
    mix_term = jnp.einsum("ne,nd->ed", attended, grad_rows, preferred_element_type=jnp.float32)
    query_back, key_back, value_back = attention_backward(
        queries,
        key_rows,
        value_rows,
        seq_start,
        log_total,
        grad_attended.reshape(row_count, heads_here, head_size),
        block_rows,
    )
    query_back = rotate(query_back, positions, -1.0).reshape(row_count, local_width)
    key_back = rotate(key_back, positions, -1.0).reshape(row_count, local_width)
    grad_projected = jnp.stack(
        [query_back, key_back, value_back.reshape(row_count, local_width)], axis=1
    ).astype(jnp.bfloat16)
    joined_term = jnp.einsum(
        "nd,nch->dch", first_rows, grad_projected, preferred_element_type=jnp.float32
    )
    joined_bias_term = jnp.sum(grad_projected, axis=0, dtype=jnp.float32).reshape(
        3, heads_here, head_size
    )
    grad_first = jnp.einsum(
        "nch,dch->nd", grad_projected, joined_again, preferred_element_type=jnp.float32
    )
    grad_local = cotangent.astype(jnp.float32)
    first_sum, second_sum = (
        lax.psum_scatter(
            grad_first.astype(jnp.bfloat16), "tensor", scatter_dimension=0, tiled=True
        ).astype(jnp.float32),
        lax.psum_scatter(
            grad_second.astype(jnp.bfloat16), "tensor", scatter_dimension=0, tiled=True
        ).astype(jnp.float32),
    )
    _, norm_back = jax.vjp(both_norms, local_f, gain_rows, shift_rows)
    grad_norm_in, gain_term, shift_term = norm_back((first_sum, second_sum))
    input_grad = grad_local + grad_norm_in
    column_sums = jnp.sum(grad_local, axis=0)
    shift_term = jnp.concatenate([shift_term[:2], jnp.stack([column_sums, column_sums])], axis=0)
    gains_grad, biases_grad = (
        lax.psum_scatter(gain_term, ("dp", "tensor"), scatter_dimension=1, tiled=True),
        lax.psum_scatter(shift_term, ("dp", "tensor"), scatter_dimension=1, tiled=True),
    )
    summed = (
        lax.psum_scatter(joined_term, "dp", scatter_dimension=0, tiled=True),
        lax.psum_scatter(joined_bias_term, "dp", scatter_dimension=2, tiled=True),
        lax.psum_scatter(mix_term, "dp", scatter_dimension=1, tiled=True),
        lax.psum_scatter(up_term, "dp", scatter_dimension=0, tiled=True),
        lax.psum_scatter(up_bias_term, "dp", scatter_dimension=1, tiled=True),
        lax.psum_scatter(down_term, "dp", scatter_dimension=1, tiled=True),
    )
    return (
        output,
        input_grad,
        summed[0],
        summed[1],
        summed[2],
        summed[3],
        summed[4],
        summed[5],
        gains_grad,
        biases_grad,
    )


def solution(mesh):
    in_specs = (
        P(("dp", "tensor"), None),
        P("dp"),
        P("dp", None, "tensor"),
        P(None, "tensor", "dp"),
        P("tensor", "dp"),
        P("dp", "tensor"),
        P("tensor", "dp"),
        P("tensor", "dp"),
        P(None, ("dp", "tensor")),
        P(None, ("dp", "tensor")),
        P(("dp", "tensor"), None),
    )
    out_specs = (
        P(("dp", "tensor"), None),
        P(("dp", "tensor"), None),
        P("dp", None, "tensor"),
        P(None, "tensor", "dp"),
        P("tensor", "dp"),
        P("dp", "tensor"),
        P("tensor", "dp"),
        P("tensor", "dp"),
        P(None, ("dp", "tensor")),
        P(None, ("dp", "tensor")),
    )
    return jax.shard_map(shards, mesh=mesh, in_specs=in_specs, out_specs=out_specs, check_vma=False)
```

profile of v0, /device:TPU:0, one launch (start us, length us, event | category | flops | bytes accessed | tf_op | source)
XLA Modules:
  0.0 1526.1 jit_solution(3073304048536600505)
XLA Ops:
  8.7 71.2 %all-gather = bf16[32,64,2]{1,2,0:T(2,128)(2,1)S(1)} all-gather(bf16[1,64,2]{1,2,0:T(2,128)(2,1)} %bitcast.182), channel_id=1, replica_groups=mesh['dp'=8,'tensor'=4] {'dp','tensor'}, dimensions={0}, use_global_device_ids=true | all-gather | bytes 8448 | tf_op jit(solution)/shard_map/all_gather | solution.py:152
  80.0 66.0 %all-gather.1 = bf16[32,64,4]{1,2,0:T(4,128)(2,1)S(1)} all-gather(bf16[1,64,4]{1,2,0:T(4,128)(2,1)} %bitcast.181), channel_id=1, replica_groups=mesh['dp'=8,'tensor'=4] {'dp','tensor'}, dimensions={0}, use_global_device_ids=true | all-gather | bytes 16896 | tf_op jit(solution)/shard_map/all_gather | solution.py:153
  183.8 47.5 %all-gather.10.cloned.1.call-done = bf16[1024,2048]{1,0:T(8,128)(2,1)} async-done(((bf16[256,2048]{1,0:T(8,128)(2,1)}), bf16[1024,2048]{1,0:T(8,128)(2,1)}) %all-gather.10.cloned.1.call-update) | async-done | bytes 4194320 | tf_op jit(solution)/shard_map/all_gather | solution.py:160
  231.3 47.4 %all-gather.12.cloned.1.call-done = bf16[2048,3,512]{0,2,1:T(8,128)(2,1)} async-done(((bf16[256,3,512]{0,2,1:T(8,128)(2,1)}), bf16[2048,3,512]{0,2,1:T(8,128)(2,1)}) %all-gather.12.cloned.1.call-update) | async-done | bytes 6291472 | tf_op jit(solution)/shard_map/all_gather | solution.py:143
  324.7 20.5 %while.27 = (s32[]{:T(128)}, bf16[2,512,2,256]{3,1,2,0:T(8,128)(2,1)}, f32[2,2,512]{2,1,0:T(2,128)S(1)}, s32[2]{0:T(128)S(1)}, s32[1024]{0:T(1024)S(1)}, /*index...) while((s32[]{:T(128)}, ...), condition=%wide.region_5.6_spmd, body=%wide.region_2.5_spmd.sunk | while | flops 1087897088 | bytes 26786032 | solution.py:78
  345.2 30.7 %while.28 = (s32[]{:T(128)}, f32[1024,2,256]{0,2,1:T(8,128)S(1)}, f32[1024,2,256]{0,2,1:T(8,128)}, f32[2,512,2,256]{3,1,0,2:T(8,128)}, s32[2]{0:T(128)S(1)}, /*i...) while((s32[]{:T(128)}, f32[1024,2,256]{0,2,1:T(8,128)S(1)}, ...), condition=%wide.region_12.13_spmd.clone, body=%wide.region_10.12_spmd.clone.sunk | while | flops 2704539136 | bytes 94415280 | solution.py:119
  394.5 11.4 bitcast_convert_fusion
  416.0 14.8 fusion.78
  430.8 42.9 %all-gather.20.cloned.1.call-done = bf16[2048,2048]{1,0:T(8,128)(2,1)} async-done(((bf16[2048,256]{1,0:T(8,128)(2,1)}), bf16[2048,2048]{1,0:T(8,128)(2,1)}) %all-gather.20.cloned.1.call-update) | async-done | bytes 8388624 | tf_op jit(solution)/shard_map/all_gather | solution.py:148
  473.8 33.0 %convert_reduce_fusion = (f32[2048]{0:T(1024)S(1)}, bf16[1024,2048]{1,0:T(8,128)(2,1)S(1)}, f32[1024,2048]{1,0:T(8,128)}) fusion(f32[1024,2048]{1,0:T(8,128)} %fusion.78, f32[2048]{0:T(1024)S(1)} %bitcast.166, bf16[1024,2048]{1,0:T(8,128)(2,1)} %all-gather.22.cloned.1.call-done, bf16[2048,2048]{1,0:T(8,128)(2,1)} %all-gather.20.cloned.1.call-done), kind=kOutput, calls=%fused_computation.50 | convolution fusion | flops 8747218944 | bytes 33570816 | tf_op jit(solution)/shard_map/nd,fd->nf/dot_general | solution.py:201
  508.7 10.9 convolution_convert_fusion
  532.2 12.7 fusion.79
  556.6 75.9 %reduce-scatter.22.cloned.1.call-done = bf16[256,2048]{1,0:T(8,128)(2,1)} async-done(((bf16[1024,2048]{1,0:T(8,128)(2,1)}), bf16[256,2048]{1,0:T(8,128)(2,1)}) %reduce-scatter.22.cloned.1.call-update) | async-done | bytes 1048592 | tf_op jit(solution)/shard_map/reduce_scatter | solution.py:242
  640.1 139.7 %reduce-scatter.20.cloned.1.call-done = f32[256,2048]{1,0:T(8,128)} async-done(((f32[1024,2048]{1,0:T(8,128)}), f32[256,2048]{1,0:T(8,128)}) %reduce-scatter.20.cloned.1.call-update) | async-done | bytes 2097168 | tf_op jit(solution)/shard_map/reduce_scatter | solution.py:184
  795.0 11.6 fusion.41
  806.7 15.3 %fusion.82 = f32[2048,2048]{1,0:T(8,128)} fusion(bf16[1024,2048]{1,0:T(8,128)(2,1)} %multiply_convert_fusion.1, bf16[1024,2048]{1,0:T(8,128)(2,1)} %all-gather.22.cloned.1.call-done), kind=kOutput, calls=%fused_computation.157 | convolution fusion | flops 8589934592 | bytes 25165824 | tf_op jit(solution)/shard_map/nf,nd->fd/dot_general | solution.py:202
  822.4 15.3 %fusion.81 = f32[2048,2048]{1,0:T(8,128)} fusion(bf16[1024,2048]{1,0:T(8,128)(2,1)} %all-gather.16.cloned.1.call-done, bf16[1024,2048]{1,0:T(8,128)(2,1)} %copy-done.45), kind=kOutput, calls=%fused_computation.156 | convolution fusion | flops 8589934592 | bytes 25165824 | tf_op jit(solution)/shard_map/nd,nf->df/dot_general | solution.py:205
  839.3 16.8 %reduce-scatter.36.cloned.1.call-done = f32[256,1]{1,0:T(8,128)} async-done(((f32[2048,1]{1,0:T(8,128)}), f32[256,1]{1,0:T(8,128)}) %reduce-scatter.36.cloned.1.call-update) | async-done | bytes 1040
  857.6 138.1 %reduce-scatter.38.cloned.1.call-done = f32[64,2]{1,0:T(8,128)} async-done(((f32[2048,2]{1,0:T(8,128)}), f32[64,2]{1,0:T(8,128)}) %reduce-scatter.38.cloned.1.call-update) | async-done | bytes 528
  997.1 134.3 %reduce-scatter.40.cloned.1.call-done = f32[64,4]{1,0:T(8,128)} async-done(((f32[2048,4]{1,0:T(8,128)}), f32[64,4]{1,0:T(8,128)}) %reduce-scatter.40.cloned.1.call-update) | async-done | bytes 1040
  1132.9 49.8 %reduce-scatter.28.cloned.1.call-done = f32[512,256]{1,0:T(8,128)} async-done(((f32[512,2048]{1,0:T(8,128)}), f32[512,256]{1,0:T(8,128)}) %reduce-scatter.28.cloned.1.call-update) | async-done | bytes 524304 | tf_op jit(solution)/shard_map/reduce_scatter | solution.py:258
  1182.7 96.0 %reduce-scatter.26.cloned.1.call-done = f32[256,3,512]{2,0,1:T(8,128)} async-done(((f32[2048,3,512]{2,0,1:T(8,128)}), f32[256,3,512]{2,0,1:T(8,128)}) %reduce-scatter.26.cloned.1.call-update) | async-done | bytes 1572880 | tf_op jit(solution)/shard_map/reduce_scatter | solution.py:256
  1278.8 120.0 %reduce-scatter.32.cloned.1.call-done = f32[2048,256]{1,0:T(8,128)} async-done(((f32[2048,2048]{1,0:T(8,128)}), f32[2048,256]{1,0:T(8,128)}) %reduce-scatter.32.cloned.1.call-update) | async-done | bytes 2097168 | tf_op jit(solution)/shard_map/reduce_scatter | solution.py:261
  1398.8 120.2 %reduce-scatter.30.cloned.1.call-done = f32[256,2048]{1,0:T(8,128)} async-done(((f32[2048,2048]{1,0:T(8,128)}), f32[256,2048]{1,0:T(8,128)}) %reduce-scatter.30.cloned.1.call-update) | async-done | bytes 2097168 | tf_op jit(solution)/shard_map/reduce_scatter | solution.py:259
  (275 shorter events, 211.5 us)
Async XLA Ops:
  7.2 143.3 %copy-start.1 = (bf16[256,2048]{1,0:T(8,128)(2,1)S(1)}, bf16[256,2048]{1,0:T(8,128)(2,1)}, u32[]{:S(2)}) copy-start(bf16[256,2048]{1,0:T(8,128)(2,1)} %param.15) | copy-start | bytes 3145732
  7.2 145.4 %copy-start.28 = (bf16[256,3,512]{2,0,1:T(8,128)(2,1)S(1)}, bf16[256,3,512]{2,0,1:T(8,128)(2,1)}, u32[]{:S(2)}) copy-start(bf16[256,3,512]{2,0,1:T(8,128)(2,1)} %param.17) | copy-start | bytes 2359300
  7.2 170.4 %all-gather.14.cloned.1.call-start = ((), (), s32[]{:S(2)}) async-start(), calls=%async_computation.13 | async-start | bytes 2359296 | tf_op jit(solution)/shard_map/all_gather | solution.py:145
  7.9 169.6 %all-gather.22.cloned.1.call-start = ((), (), s32[]{:S(2)}) async-start(), calls=%async_computation.18 | async-start | bytes 5242880 | tf_op jit(solution)/shard_map/all_gather | solution.py:191
  8.7 222.6 %all-gather.10.cloned.1.call-start = ((), (), s32[]{:S(2)}) async-start(), calls=%async_computation.11 | async-start | bytes 5242880 | tf_op jit(solution)/shard_map/all_gather | solution.py:160
  152.5 126.2 %all-gather.12.cloned.1.call-start = ((), (), s32[]{:S(2)}) async-start(), calls=%async_computation.12 | async-start | bytes 7077888 | tf_op jit(solution)/shard_map/all_gather | solution.py:143
  153.8 252.2 %all-gather.16.cloned.1.call-start = ((), (), s32[]{:S(2)}) async-start(), calls=%async_computation.14 | async-start | bytes 5242880 | tf_op jit(solution)/shard_map/all_gather | solution.py:161
  154.4 261.6 %all-gather.18.cloned.1.call-start = ((), (), s32[]{:S(2)}) async-start(), calls=%async_computation.15 | async-start | bytes 9437184 | tf_op jit(solution)/shard_map/all_gather | solution.py:146
  155.0 318.8 %all-gather.20.cloned.1.call-start = ((), (), s32[]{:S(2)}) async-start(), calls=%async_computation.16 | async-start | bytes 9437184 | tf_op jit(solution)/shard_map/all_gather | solution.py:148
  155.7 400.8 %reduce-scatter.24.cloned.1.call-start = ((), (), s32[]{:S(2)}) async-start(), calls=%async_computation.20 | async-start | bytes 5242880 | tf_op jit(solution)/shard_map/reduce_scatter | solution.py:239
  405.9 226.6 %reduce-scatter.22.cloned.1.call-start = ((), (), s32[]{:S(2)}) async-start(), calls=%async_computation.19 | async-start | bytes 5242880 | tf_op jit(solution)/shard_map/reduce_scatter | solution.py:242
  519.7 260.2 %reduce-scatter.20.cloned.1.call-start = ((), (), s32[]{:S(2)}) async-start(), calls=%async_computation.17 | async-start | bytes 10485760 | tf_op jit(solution)/shard_map/reduce_scatter | solution.py:184
  550.7 84.6 %copy-start.39 = (f32[256]{0:T(256)S(1)}, f32[256]{0:T(256)}, u32[]{:S(2)}) copy-start(f32[256]{0:T(256)} %copy-done.38) | copy-start | bytes 3076
  550.7 287.1 %reduce-scatter.34.cloned.1.call-start = ((), (), s32[]{:S(2)}) async-start(), calls=%async_computation.25 | async-start | bytes 147456
  555.0 301.0 %reduce-scatter.36.cloned.1.call-start = ((), (), s32[]{:S(2)}) async-start(), calls=%async_computation.26 | async-start | bytes 1179648
  556.5 223.4 %copy-start.36 = (f32[1,2048]{1,0:T(1,128)S(1)}, f32[1,2048]{1,0:T(1,128)}, u32[]{:S(2)}) copy-start(f32[1,2048]{1,0:T(1,128)} %get-tuple-element.328) | copy-start | bytes 24580
  556.5 223.4 %copy-start.37 = (f32[1,2048]{1,0:T(1,128)S(1)}, f32[1,2048]{1,0:T(1,128)}, u32[]{:S(2)}) copy-start(f32[1,2048]{1,0:T(1,128)} %get-tuple-element.329) | copy-start | bytes 24580
  556.5 439.3 %reduce-scatter.38.cloned.1.call-start = ((), (), s32[]{:S(2)}) async-start(), calls=%async_computation.27 | async-start | bytes 1081344
  556.6 223.3 %copy-start.4 = (bf16[256,2048]{1,0:T(8,128)(2,1)S(1)}, bf16[256,2048]{1,0:T(8,128)(2,1)}, u32[]{:S(2)}) copy-start(bf16[256,2048]{1,0:T(8,128)(2,1)} %reduce-scatter.24.cloned.1.call-done) | copy-start | bytes 3145732
  640.1 491.4 %reduce-scatter.40.cloned.1.call-start = ((), (), s32[]{:S(2)}) async-start(), calls=%async_computation.28 | async-start | bytes 1081344
  786.3 396.4 %reduce-scatter.28.cloned.1.call-start = ((), (), s32[]{:S(2)}) async-start(), calls=%async_computation.22 | async-start | bytes 4718592 | tf_op jit(solution)/shard_map/reduce_scatter | solution.py:258
  793.2 485.6 %reduce-scatter.26.cloned.1.call-start = ((), (), s32[]{:S(2)}) async-start(), calls=%async_computation.21 | async-start | bytes 14155776 | tf_op jit(solution)/shard_map/reduce_scatter | solution.py:256
  806.7 592.1 %reduce-scatter.32.cloned.1.call-start = ((), (), s32[]{:S(2)}) async-start(), calls=%async_computation.24 | async-start | bytes 18874368 | tf_op jit(solution)/shard_map/reduce_scatter | solution.py:261
  822.1 696.9 %reduce-scatter.30.cloned.1.call-start = ((), (), s32[]{:S(2)}) async-start(), calls=%async_computation.23 | async-start | bytes 18874368 | tf_op jit(solution)/shard_map/reduce_scatter | solution.py:259
  (49 other events, 689.5 us)
Sparse Core Ops, SparseCore 0:
  9.9 30.8 all-gather.13
  42.3 81.0 all-gather.21
  152.7 78.5 all-gather.9
  233.6 45.0 all-gather.11
  280.7 80.7 all-gather.15
  363.2 52.7 all-gather.17
  417.9 55.8 all-gather.19
  476.0 76.7 reduce-scatter.23
  555.2 77.2 reduce-scatter.21
  634.7 145.1 reduce-scatter.19
  782.9 34.1 reduce-scatter.33
  820.1 35.9 reduce-scatter.35
  858.3 137.3 reduce-scatter.37
  997.9 133.5 reduce-scatter.39
  1135.3 47.4 reduce-scatter.27
  1186.7 92.0 reduce-scatter.25
  1282.8 115.9 reduce-scatter.31
  1402.8 116.1 reduce-scatter.29
where the time goes:
time: 1530 us
  waiting for transfers between devices  1040 us (68%)
  matrix products  177 us (12%)
  blocking collectives  155 us (10%)
  local copies, waits for them, and re-layouts  69 us (5%)
  other arithmetic  58 us (4%)
    unnamed x22, waiting for transfers between devices  293 us
    reduce_scatter x1, waiting for transfers between devices, shards(): lax.psum_scatter(attn_part + jnp.dot(activated, back_weight, preferred_el...  140 us
    reduce_scatter x1, waiting for transfers between devices, shards(): lax.psum_scatter(up_term, 'dp', scatter_dimension=0, tiled=True)  120 us
    reduce_scatter x1, waiting for transfers between devices, shards(): lax.psum_scatter(down_term, 'dp', scatter_dimension=1, tiled=True)  120 us
    reduce_scatter x1, waiting for transfers between devices, shards(): lax.psum_scatter(joined_term, 'dp', scatter_dimension=0, tiled=True)  96 us
    reduce_scatter x1, waiting for transfers between devices, shards(): lax.psum_scatter(grad_second.astype(jnp.bfloat16), 'tensor', scatter_dime...  75.9 us
    all_gather x1, blocking collectives, shards(): lax.all_gather(norm_gains, ('dp', 'tensor'), axis=1, tiled=True)  71.2 us
    all_gather x1, blocking collectives, shards(): lax.all_gather(biases, ('dp', 'tensor'), axis=1, tiled=True)  66 us
  transfers between devices with their start and end apart: 18, of which 13 were waited for; matrix products, arithmetic and copies ran while one was open for 19% of the time, Pallas kernels for 0%

commit v1 on v0

--- a/solution.py
+++ b/solution.py
@@ -6,6 +6,28 @@
 ROT = 64
 EPSILON = 1e-05
 ROTARY_BASE = 10000.0
+
+
+def laid_out(tiles, dim):
+    tiles = jnp.moveaxis(tiles, 0, dim)
+    lengths = tiles.shape
+    return tiles.reshape(*lengths[:dim], lengths[dim] * lengths[dim + 1], *lengths[dim + 2 :])
+
+
+def doubled(x, axis):
+    length = lax.axis_size(axis)
+    parts = x[None]
+    for level in range(length.bit_length() - 1):
+        bit = 1 << level
+        other = lax.ppermute(parts, axis, [(i, i ^ bit) for i in range(length)])
+        both = jnp.stack([parts, other])
+        upper = lax.axis_index(axis) >> level & 1
+        parts = jnp.where(upper == 0, both, both[::-1]).reshape(-1, *x.shape)
+    return parts
+
+
+def gather_by_bits(x, axis, dim):
+    return laid_out(doubled(x, axis), dim)
 
 
 def layer_norm(values, gain_row, shift_row):
@@ -145,7 +167,7 @@
         lax.all_gather(out_weight, "dp", axis=1, tiled=True),
         lax.all_gather(up_weight, "dp", axis=0, tiled=True),
         lax.all_gather(up_bias, "dp", axis=1, tiled=True),
-        lax.all_gather(down_weight, "dp", axis=1, tiled=True),
+        gather_by_bits(down_weight, "dp", 1),
     )
     joined_weight, joined_bias, mix_weight, hidden_weight, hidden_bias, back_weight = gathered
     gain_rows, shift_rows = (

time: 1530 us -> 1560 us (1.020)
  waiting for transfers between devices: 1040 us -> 985 us
  blocking collectives: 155 us -> 197 us
  other arithmetic: 58 us -> 82.4 us
  matrix products: 177 us -> 193 us
    all_gather x1, waiting for transfers between devices: 47.5 us -> 0.01 us  [shards(): lax.all_gather(first_local.astype(jnp.bfloat16), 'tensor', axis=0, tiled=...]
    all_gather x1, blocking collectives: 9.5 us -> 51.3 us  [shards(): lax.all_gather(proj_bias, 'dp', axis=2, tiled=True)]
    reduce_scatter x1, waiting for transfers between devices: 75.9 us -> 45.1 us  [shards(): lax.psum_scatter(grad_second.astype(jnp.bfloat16), 'tensor', scatter_dime...]
    select_n x0 -> x2, other arithmetic: none -> 17.2 us  [doubled(): parts = jnp.where(upper == 0, both, both[::-1]).reshape(-1, *x.shape)]
    unnamed x94 -> x102, local copies, waits for them, and re-layouts: 34.8 us -> 29.3 us
  transfers between devices with their start and end apart: 18 -> 21, of which waited for: 13 -> 13; matrix products, arithmetic and copies ran while one was open for 19% -> 21% of each run, Pallas kernels for 0% -> 0%
where the time goes in v1:
time: 1560 us; the launch traced here: 1550 us
  waiting for transfers between devices  985 us (63%)
  blocking collectives  197 us (13%)
  matrix products  193 us (12%)
  other arithmetic  82.4 us (5%)
  local copies, waits for them, and re-layouts  68.2 us (4%)
    unnamed x22, waiting for transfers between devices  292 us
    reduce_scatter x1, waiting for transfers between devices, shards(): lax.psum_scatter(attn_part + jnp.dot(activated, back_weight, preferred_el...  140 us
    reduce_scatter x1, waiting for transfers between devices, shards(): lax.psum_scatter(up_term, 'dp', scatter_dimension=0, tiled=True)  120 us
    reduce_scatter x1, waiting for transfers between devices, shards(): lax.psum_scatter(down_term, 'dp', scatter_dimension=1, tiled=True)  120 us
    reduce_scatter x1, waiting for transfers between devices, shards(): lax.psum_scatter(joined_term, 'dp', scatter_dimension=0, tiled=True)  96 us
    all_gather x1, blocking collectives, shards(): lax.all_gather(norm_gains, ('dp', 'tensor'), axis=1, tiled=True)  71.2 us
    all_gather x1, blocking collectives, shards(): lax.all_gather(biases, ('dp', 'tensor'), axis=1, tiled=True)  66 us
    all_gather x1, waiting for transfers between devices, shards(): lax.all_gather(proj_weight, 'dp', axis=0, tiled=True)  61 us
  transfers between devices with their start and end apart: 21, of which 13 were waited for; matrix products, arithmetic and copies ran while one was open for 21% of the time, Pallas kernels for 0%

profile of v1, /device:TPU:0, one launch (start us, length us, event | category | flops | bytes accessed | tf_op | source)
XLA Modules:
  0.0 1551.0 jit_solution(11538713949443641602)
XLA Ops:
  8.7 71.2 %all-gather = bf16[32,64,2]{1,2,0:T(2,128)(2,1)S(1)} all-gather(bf16[1,64,2]{1,2,0:T(2,128)(2,1)} %bitcast.204), channel_id=1, replica_groups=mesh['dp'=8,'tensor'=4] {'dp','tensor'}, dimensions={0}, use_global_device_ids=true | all-gather | bytes 8448 | tf_op jit(solution)/shard_map/all_gather | solution.py:174
  80.0 66.0 %all-gather.1 = bf16[32,64,4]{1,2,0:T(4,128)(2,1)S(1)} all-gather(bf16[1,64,4]{1,2,0:T(4,128)(2,1)} %bitcast.203), channel_id=1, replica_groups=mesh['dp'=8,'tensor'=4] {'dp','tensor'}, dimensions={0}, use_global_device_ids=true | all-gather | bytes 16896 | tf_op jit(solution)/shard_map/all_gather | solution.py:175
  160.1 51.3 %all_gather.40 = bf16[3,2,256]{0,1,2:T(2,128)(2,1)S(1)} all-gather(bf16[3,2,32]{0,1,2:T(2,128)(2,1)S(1)} %copy.125), channel_id=1, replica_groups=mesh['dp'=8,'tensor'=4] {'dp'}, dimensions={2}, use_global_device_ids=true | all-gather | bytes 3456 | tf_op jit(solution)/shard_map/all_gather | solution.py:166
  242.6 61.0 %all-gather.12.cloned.1.call-done = bf16[2048,3,512]{0,2,1:T(8,128)(2,1)} async-done(((bf16[256,3,512]{0,2,1:T(8,128)(2,1)}), bf16[2048,3,512]{0,2,1:T(8,128)(2,1)}) %all-gather.12.cloned.1.call-update) | async-done | bytes 6291472 | tf_op jit(solution)/shard_map/all_gather | solution.py:165
  333.4 19.8 %while.27 = (s32[]{:T(128)}, bf16[2,512,2,256]{3,1,2,0:T(8,128)(2,1)}, f32[2,2,512]{2,1,0:T(2,128)S(1)}, s32[2]{0:T(128)S(1)}, s32[1024]{0:T(1024)S(1)}, /*index...) while((s32[]{:T(128)}, ...), condition=%wide.region_5.6_spmd, body=%wide.region_2.5_spmd.sunk | while | flops 1087897088 | bytes 18397868 | solution.py:100
  353.3 40.5 %while.28 = (s32[]{:T(128)}, f32[1024,2,256]{0,2,1:T(8,128)}, f32[1024,2,256]{0,2,1:T(8,128)}, f32[2,512,2,256]{3,1,0,2:T(8,128)}, s32[2]{0:T(128)S(1)}, /*index...) while((s32[]{:T(128)}, f32[1024,2,256]{0,2,1:T(8,128)}, ...), condition=%wide.region_12.13_spmd.clone, body=%wide.region_10.12_spmd.clone.sunk | while | flops 2704539136 | bytes 123775488 | solution.py:141
  413.0 12.7 bitcast_convert_fusion
  425.8 15.1 all-gather.18.cloned.1.call-done
  440.9 14.6 fusion.81
  455.5 43.2 %all-gather.22.cloned.1.call-done = bf16[2048,2048]{1,0:T(8,128)(2,1)} async-done(((bf16[2048,256]{1,0:T(8,128)(2,1)}), bf16[2048,2048]{1,0:T(8,128)(2,1)}) %all-gather.22.cloned.1.call-update) | async-done | bytes 8388624 | tf_op jit(solution)/shard_map/all_gather | solution.py:220
  498.7 33.1 %convert_reduce_fusion = (f32[2048]{0:T(1024)S(1)}, bf16[1024,2048]{1,0:T(8,128)(2,1)S(1)}, f32[1024,2048]{1,0:T(8,128)}) fusion(f32[1024,2048]{1,0:T(8,128)} %fusion.81, f32[2048]{0:T(1024)S(1)} %bitcast.188, bf16[1024,2048]{1,0:T(8,128)(2,1)} %all-gather.20.cloned.1.call-done, bf16[2048,2048]{1,0:T(8,128)(2,1)} %all-gather.22.cloned.1.call-done), kind=kOutput, calls=%fused_computation.52 | convolution fusion | flops 8747218944 | bytes 33570816 | tf_op jit(solution)/shard_map/nd,fd->nf/dot_general | solution.py:223
  558.6 14.3 reverse_select_fusion
  591.6 14.7 convolution_add_fusion
  612.3 45.1 %reduce-scatter.22.cloned.1.call-done = bf16[256,2048]{1,0:T(8,128)(2,1)} async-done(((bf16[1024,2048]{1,0:T(8,128)(2,1)}), bf16[256,2048]{1,0:T(8,128)(2,1)}) %reduce-scatter.22.cloned.1.call-update) | async-done | bytes 1048592 | tf_op jit(solution)/shard_map/reduce_scatter | solution.py:264
  665.2 139.6 %reduce-scatter.20.cloned.1.call-done = f32[256,2048]{1,0:T(8,128)} async-done(((f32[1024,2048]{1,0:T(8,128)}), f32[256,2048]{1,0:T(8,128)}) %reduce-scatter.20.cloned.1.call-update) | async-done | bytes 2097168 | tf_op jit(solution)/shard_map/reduce_scatter | solution.py:206
  832.0 15.2 fusion.84
  847.3 15.2 fusion.83
  864.1 16.9 %reduce-scatter.36.cloned.1.call-done = f32[256,1]{1,0:T(8,128)} async-done(((f32[2048,1]{1,0:T(8,128)}), f32[256,1]{1,0:T(8,128)}) %reduce-scatter.36.cloned.1.call-update) | async-done | bytes 1040
  882.6 138.1 %reduce-scatter.38.cloned.1.call-done = f32[64,2]{1,0:T(8,128)} async-done(((f32[2048,2]{1,0:T(8,128)}), f32[64,2]{1,0:T(8,128)}) %reduce-scatter.38.cloned.1.call-update) | async-done | bytes 528
  1022.1 134.5 %reduce-scatter.40.cloned.1.call-done = f32[64,4]{1,0:T(8,128)} async-done(((f32[2048,4]{1,0:T(8,128)}), f32[64,4]{1,0:T(8,128)}) %reduce-scatter.40.cloned.1.call-update) | async-done | bytes 1040
  1158.0 49.7 %reduce-scatter.28.cloned.1.call-done = f32[512,256]{1,0:T(8,128)} async-done(((f32[512,2048]{1,0:T(8,128)}), f32[512,256]{1,0:T(8,128)}) %reduce-scatter.28.cloned.1.call-update) | async-done | bytes 524304 | tf_op jit(solution)/shard_map/reduce_scatter | solution.py:280
  1207.7 96.0 %reduce-scatter.26.cloned.1.call-done = f32[256,3,512]{2,0,1:T(8,128)} async-done(((f32[2048,3,512]{2,0,1:T(8,128)}), f32[256,3,512]{2,0,1:T(8,128)}) %reduce-scatter.26.cloned.1.call-update) | async-done | bytes 1572880 | tf_op jit(solution)/shard_map/reduce_scatter | solution.py:278
  1303.7 120.0 %reduce-scatter.32.cloned.1.call-done = f32[2048,256]{1,0:T(8,128)} async-done(((f32[2048,2048]{1,0:T(8,128)}), f32[2048,256]{1,0:T(8,128)}) %reduce-scatter.32.cloned.1.call-update) | async-done | bytes 2097168 | tf_op jit(solution)/shard_map/reduce_scatter | solution.py:283
  1423.7 120.2 %reduce-scatter.30.cloned.1.call-done = f32[256,2048]{1,0:T(8,128)} async-done(((f32[2048,2048]{1,0:T(8,128)}), f32[256,2048]{1,0:T(8,128)}) %reduce-scatter.30.cloned.1.call-update) | async-done | bytes 2097168 | tf_op jit(solution)/shard_map/reduce_scatter | solution.py:281
  (301 shorter events, 239.5 us)
Async XLA Ops:
  7.2 228.9 %all-gather.14.cloned.1.call-start = ((), (), s32[]{:S(2)}) async-start(), calls=%async_computation.13 | async-start | bytes 2359296 | tf_op jit(solution)/shard_map/all_gather | solution.py:167
  7.9 228.2 %all-gather.20.cloned.1.call-start = ((), (), s32[]{:S(2)}) async-start(), calls=%async_computation.17 | async-start | bytes 5242880 | tf_op jit(solution)/shard_map/all_gather | solution.py:213
  8.7 233.9 %all-gather.10.cloned.1.call-start = ((), (), s32[]{:S(2)}) async-start(), calls=%async_computation.11 | async-start | bytes 5242880 | tf_op jit(solution)/shard_map/all_gather | solution.py:182
  152.6 151.1 %all-gather.12.cloned.1.call-start = ((), (), s32[]{:S(2)}) async-start(), calls=%async_computation.12 | async-start | bytes 7077888 | tf_op jit(solution)/shard_map/all_gather | solution.py:165
  153.8 272.1 %all-gather.16.cloned.1.call-start = ((), (), s32[]{:S(2)}) async-start(), calls=%async_computation.14 | async-start | bytes 5242880 | tf_op jit(solution)/shard_map/all_gather | solution.py:183
  154.4 286.5 %all-gather.18.cloned.1.call-start = ((), (), s32[]{:S(2)}) async-start(), calls=%async_computation.15 | async-start | bytes 9437184 | tf_op jit(solution)/shard_map/all_gather | solution.py:168
  155.0 343.7 %all-gather.22.cloned.1.call-start = ((), (), s32[]{:S(2)}) async-start(), calls=%async_computation.18 | async-start | bytes 9437184 | tf_op jit(solution)/shard_map/all_gather | solution.py:220
  155.0 2.7 collective-permute-start
  159.8 64.3 %collective-permute-start.1 = (bf16[2,2048,256]{2,1,0:T(8,128)(2,1)}, bf16[2,2048,256]{2,1,0:T(8,128)(2,1)}, u32[]{:S(2)}, u32[]{:S(2)}) collective-permute-start(bf16[2,2048,256]{2,1,0:T(8,128)(2,1)} %get-tuple-element.316), channel_id=1, source_target_pairs={{0,8},{4,12},{8,0},{12,4},{16,24},{20,28},{24,16},{28,20},{1,9},{5... | collective-permute-start | bytes 6291464 | tf_op jit(solution)/shard_map/ppermute | solution.py:22
  159.9 452.4 %reduce-scatter.24.cloned.1.call-start = ((), (), s32[]{:S(2)}) async-start(), calls=%async_computation.20 | async-start | bytes 5242880 | tf_op jit(solution)/shard_map/reduce_scatter | solution.py:261
  235.3 315.7 %collective-permute-start.2 = (bf16[4,2048,256]{1,2,0:T(8,128)(2,1)}, bf16[4,2048,256]{1,2,0:T(8,128)(2,1)}, u32[]{:S(2)}, u32[]{:S(2)}) collective-permute-start(bf16[4,2048,256]{1,2,0:T(8,128)(2,1)} %copy.135), channel_id=1, source_target_pairs={{0,16},{4,20},{8,24},{12,28},{16,0},{20,4},{24,8},{28,12},{1,17},{... | collective-permute-start | bytes 12582920 | tf_op jit(solution)/shard_map/ppermute | solution.py:22
  425.8 231.6 %reduce-scatter.22.cloned.1.call-start = ((), (), s32[]{:S(2)}) async-start(), calls=%async_computation.19 | async-start | bytes 5242880 | tf_op jit(solution)/shard_map/reduce_scatter | solution.py:264
  544.3 260.5 %reduce-scatter.20.cloned.1.call-start = ((), (), s32[]{:S(2)}) async-start(), calls=%async_computation.16 | async-start | bytes 10485760 | tf_op jit(solution)/shard_map/reduce_scatter | solution.py:206
  606.4 256.2 %reduce-scatter.34.cloned.1.call-start = ((), (), s32[]{:S(2)}) async-start(), calls=%async_computation.25 | async-start | bytes 147456
  610.8 270.3 %reduce-scatter.36.cloned.1.call-start = ((), (), s32[]{:S(2)}) async-start(), calls=%async_computation.26 | async-start | bytes 1179648
  612.2 192.6 %copy-start.40 = (f32[1,2048]{1,0:T(1,128)S(1)}, f32[1,2048]{1,0:T(1,128)}, u32[]{:S(2)}) copy-start(f32[1,2048]{1,0:T(1,128)} %get-tuple-element.330) | copy-start | bytes 24580
  612.2 192.6 %copy-start.41 = (f32[1,2048]{1,0:T(1,128)S(1)}, f32[1,2048]{1,0:T(1,128)}, u32[]{:S(2)}) copy-start(f32[1,2048]{1,0:T(1,128)} %get-tuple-element.331) | copy-start | bytes 24580
  612.2 408.5 %reduce-scatter.38.cloned.1.call-start = ((), (), s32[]{:S(2)}) async-start(), calls=%async_computation.27 | async-start | bytes 1081344
  612.3 192.5 %copy-start.8 = (bf16[256,2048]{1,0:T(8,128)(2,1)S(1)}, bf16[256,2048]{1,0:T(8,128)(2,1)}, u32[]{:S(2)}) copy-start(bf16[256,2048]{1,0:T(8,128)(2,1)} %reduce-scatter.24.cloned.1.call-done) | copy-start | bytes 3145732
  665.1 491.5 %reduce-scatter.40.cloned.1.call-start = ((), (), s32[]{:S(2)}) async-start(), calls=%async_computation.28 | async-start | bytes 1081344
  811.3 396.4 %reduce-scatter.28.cloned.1.call-start = ((), (), s32[]{:S(2)}) async-start(), calls=%async_computation.22 | async-start | bytes 4718592 | tf_op jit(solution)/shard_map/reduce_scatter | solution.py:280
  818.2 485.5 %reduce-scatter.26.cloned.1.call-start = ((), (), s32[]{:S(2)}) async-start(), calls=%async_computation.21 | async-start | bytes 14155776 | tf_op jit(solution)/shard_map/reduce_scatter | solution.py:278
  832.0 591.7 %reduce-scatter.32.cloned.1.call-start = ((), (), s32[]{:S(2)}) async-start(), calls=%async_computation.24 | async-start | bytes 18874368 | tf_op jit(solution)/shard_map/reduce_scatter | solution.py:283
  847.3 696.7 %reduce-scatter.30.cloned.1.call-start = ((), (), s32[]{:S(2)}) async-start(), calls=%async_computation.23 | async-start | bytes 18874368 | tf_op jit(solution)/shard_map/reduce_scatter | solution.py:281
  (58 other events, 1180.8 us)
Sparse Core Ops, SparseCore 0:
  9.9 30.8 all-gather.13
  42.3 81.0 all-gather.19
  152.7 78.5 all-gather.9
  233.0 70.5 all-gather.11
  305.6 80.7 all-gather.15
  388.1 52.7 all-gather.17
  442.8 55.8 all-gather.21
  501.0 76.7 reduce-scatter.23
  580.1 77.2 reduce-scatter.21
  659.6 145.1 reduce-scatter.19
  807.8 34.1 reduce-scatter.33
  845.0 35.9 reduce-scatter.35
  883.3 137.3 reduce-scatter.37
  1022.8 133.7 reduce-scatter.39
  1160.3 47.2 reduce-scatter.27
  1211.6 92.0 reduce-scatter.25
  1307.7 115.9 reduce-scatter.31
  1427.7 116.1 reduce-scatter.29
